TPU v7x, 32 devices: a whole 2x2x4 slice. The times are simulated.
32 devices in a mesh: groups: 2 (over x), seq: 16 (over z, y, core).
Axes of the slice: x: 2, y: 2, z: 4, core: 2. Of those that a mesh axis runs over, the one named last changes fastest.
Arguments:
- q_fresh: bfloat16 [5120, 4096], P(('groups', 'seq')), parts along dimension 0, may hold values from -9 to 9, as said below
- k_fresh: bfloat16 [5120, 4096], P(('groups', 'seq')), parts along dimension 0, may hold values from -5.6 to 5.6, as said below
- v_fresh: bfloat16 [5120, 4096], P(('groups', 'seq')), parts along dimension 0, may hold values from -6 to 6
- k_stale: bfloat16 [5120, 4096], P('groups', 'seq'), parts along dimension 0, may hold values from -5.59375 to 5.59375
- v_stale: bfloat16 [5120, 4096], P('groups', 'seq'), parts along dimension 0, may hold values from -6 to 6
- rank: int32 [10], P('groups'), parts along dimension 0, may hold values from 0 to 4, each once
- ends: int32 [10], P('groups'), parts along dimension 0, may hold values from 512 to 2560, as said below
Outputs:
- attended: bfloat16 [5120, 4096], P(('groups', 'seq')), parts along dimension 0
There are 2 independent parts, one for each index of `groups`. A program takes and returns all parts, laid end to end along the dimension named above; each array names one. Nothing has to cross between parts.
Inputs may be any that keep to these rules, and one draw needn't show every extreme that they name: `q_fresh`: queries of both draws lie within this range. `k_fresh`: keys of both draws lie within this range. Multiples of 512, never falling along the patches, ends[p] >= (p + 1) * 512; the first equals 512, the last equals 2560.
All inputs are finite; a program needn't handle non-finite values.
Results may differ from a plain program's by a relative error of at most 0.0036.
Values may be sent and summed in bfloat16 or wider, within the bound.
No kernel may reach another device: no remote copies, remote signals or barrier semaphores. Data moves between devices by JAX's collectives and lax.ppermute only.
A program may use at most 64 MiB of HBM per device.

v0:
```python
import math
import jax
import jax.numpy as jnp
from jax import lax
from jax.sharding import PartitionSpec as P

HEAD_DIM = 128
PATCH = 512


def shards(q_fresh, k_fresh, v_fresh, k_stale, v_stale, rank, ends):
    queries, keys_new, values_new = (
        lax.all_to_all(q_fresh, "seq", split_axis=1, concat_axis=0, tiled=True),
        lax.all_to_all(k_fresh, "seq", split_axis=1, concat_axis=0, tiled=True),
        lax.all_to_all(v_fresh, "seq", split_axis=1, concat_axis=0, tiled=True),
    )
    total_rows = queries.shape[0]
    width = queries.shape[1]
    heads_here = width // HEAD_DIM
    patch_count = rank.shape[0]
    scale = 1.0 / math.sqrt(HEAD_DIM)
    key_patch = jnp.arange(total_rows, dtype=jnp.int32) // PATCH
    hits = key_patch[:, None] == jnp.arange(patch_count, dtype=jnp.int32)[None, :]
    key_rank = jnp.sum(jnp.where(hits, rank[None, :], 0), axis=1)
    positions = jnp.arange(total_rows, dtype=jnp.int32)

    def split_heads(array):
        return array.reshape(array.shape[0], heads_here, HEAD_DIM)

    def one_patch(index):
        block = split_heads(lax.dynamic_slice_in_dim(queries, index * PATCH, PATCH, 0))
        my_rank = rank[index]
        limit = ends[index]
        fresh = (key_rank <= my_rank)[:, None]
        keys = split_heads(jnp.where(fresh, keys_new, k_stale))
        values = split_heads(jnp.where(fresh, values_new, v_stale))
        score = jnp.einsum("qhd,khd->hqk", block, keys, preferred_element_type=jnp.float32) * scale
        score = jnp.where((positions < limit)[None, None, :], score, -jnp.inf)
        top = jnp.max(score, axis=2, keepdims=True)
        weight = jnp.exp(score - top)
        denominator = jnp.sum(weight, axis=2)
        mixed = jnp.einsum(
            "hqk,khd->qhd", weight.astype(jnp.bfloat16), values, preferred_element_type=jnp.float32
        )
        result = mixed / jnp.transpose(denominator)[:, :, None]
        return result.reshape(PATCH, width).astype(jnp.bfloat16)

    pieces = lax.map(one_patch, jnp.arange(patch_count, dtype=jnp.int32))
    gathered = pieces.reshape(total_rows, width)
    return lax.all_to_all(gathered, "seq", split_axis=0, concat_axis=1, tiled=True)


def solution(mesh):
    return jax.shard_map(
        shards,
        mesh=mesh,
        in_specs=(
            P(("groups", "seq"), None),
            P(("groups", "seq"), None),
            P(("groups", "seq"), None),
            P("groups", "seq"),
            P("groups", "seq"),
            P("groups"),
            P("groups"),
        ),
        out_specs=P(("groups", "seq"), None),
        check_vma=False,
    )
```

profile of v0, /device:TPU:1, one launch (start us, length us, event | category | flops | bytes accessed | tf_op | source)
XLA Modules:
  0.0 222.0 jit_solution(114587770779463893)
XLA Ops:
  0.0 2.5 %copy.83 = bf16[20,16,8,256]{3,2,0,1:T(8,128)(2,1)} copy(bf16[20,16,8,256]{3,2,1,0:T(8,128)(2,1)} %bitcast.75) | data formatting | bytes 2621440 | tf_op jit(solution)/shard_map/all_to_all | solution.py:15
  2.5 7.5 %all-to-all-start = ((bf16[160,16,256]{2,0,1:T(8,128)(2,1)}), bf16[160,16,256]{2,0,1:T(8,128)(2,1)S(1)}, u32[]{:S(2)}, u32[]{:S(2)}) async-start(bf16[160,16,256]{2,0,1:T(8,128)(2,1)} %bitcast.41), calls=%async_computation | async-start | bytes 2621440 | tf_op jit(solution)/shard_map/all_to_all | solution.py:15
  11.2 26.6 %all-to-all-done = bf16[160,16,256]{2,0,1:T(8,128)(2,1)S(1)} async-done(((bf16[160,16,256]{2,0,1:T(8,128)(2,1)}), bf16[160,16,256]{2,0,1:T(8,128)(2,1)S(1)}, u32[]{:S(2)}, u32[]{:S(2)}) %all-to-all-start) | async-done | bytes 1310752 | tf_op jit(solution)/shard_map/all_to_all | solution.py:15
  37.8 7.5 %all-to-all-start.2 = ((bf16[160,16,256]{2,0,1:T(8,128)(2,1)}), bf16[160,16,256]{2,0,1:T(8,128)(2,1)S(1)}, u32[]{:S(2)}, u32[]{:S(2)}) async-start(bf16[160,16,256]{2,0,1:T(8,128)(2,1)} %bitcast.73), calls=%async_computation.2 | async-start | bytes 2621440 | tf_op jit(solution)/shard_map/all_to_all | solution.py:14
  45.3 2.5 %copy.82 = bf16[20,16,8,256]{3,2,0,1:T(8,128)(2,1)} copy(bf16[20,16,8,256]{3,2,1,0:T(8,128)(2,1)} %bitcast.77) | data formatting | bytes 2621440 | tf_op jit(solution)/shard_map/all_to_all | solution.py:13
  47.8 25.3 %all-to-all-done.2 = bf16[160,16,256]{2,0,1:T(8,128)(2,1)S(1)} async-done(((bf16[160,16,256]{2,0,1:T(8,128)(2,1)}), bf16[160,16,256]{2,0,1:T(8,128)(2,1)S(1)}, u32[]{:S(2)}, u32[]{:S(2)}) %all-to-all-start.2) | async-done | bytes 1310752 | tf_op jit(solution)/shard_map/all_to_all | solution.py:14
  74.2 7.5 %all-to-all-start.1 = ((bf16[160,16,256]{2,0,1:T(8,128)(2,1)}), bf16[160,16,256]{2,0,1:T(8,128)(2,1)}, u32[]{:S(2)}, u32[]{:S(2)}) async-start(bf16[160,16,256]{2,0,1:T(8,128)(2,1)} %bitcast.72), calls=%async_computation.1 | async-start | bytes 2621440 | tf_op jit(solution)/shard_map/all_to_all | solution.py:13
  81.7 2.4 %copy.63 = bf16[2560,256]{0,1:T(8,128)(2,1)} copy(bf16[2560,256]{1,0:T(8,128)(2,1)} %param.13) | data formatting | bytes 2621440
  84.1 1.6 copy.66
  85.9 1.6 copy.62
  87.5 1.6 copy.65
  89.1 20.6 %all-to-all-done.1 = bf16[160,16,256]{2,0,1:T(8,128)(2,1)} async-done(((bf16[160,16,256]{2,0,1:T(8,128)(2,1)}), bf16[160,16,256]{2,0,1:T(8,128)(2,1)}, u32[]{:S(2)}, u32[]{:S(2)}) %all-to-all-start.1) | async-done | bytes 1310752 | tf_op jit(solution)/shard_map/all_to_all | solution.py:13
  109.6 71.8 %while.11 = (s32[]{:T(128)}, bf16[5,512,256]{2,1,0:T(8,128)(2,1)}, s32[5]{0:T(128)S(1)}, s32[5]{0:T(128)S(1)}, s32[2560]{0:T(1024)S(1)}, /*index=5*/bf16[2560,25...) while((s32[]{:T(128)}, bf16[5,512,256]{2,1,0:T(8,128)(2,1)}, ...), condition=%wide.region_4.5_spmd.clone, body=%wide.region_1.4_spmd.clone.sunk | while | flops 1372589056 | bytes 49856844 | solution.py:48
  113.4 1.3 iota_compare_fusion.3
  116.4 1.7 fusion.43
  118.2 2.2 %fusion.44 = f32[2,512]{1,0:T(2,128)S(1)} fusion(f32[2,512,2560]{2,1,0:T(8,128)S(1)} %get-tuple-element.257, f32[2,512]{1,0:T(2,128)S(1)} %get-tuple-element.258, pred[2560]{0:T(1024)(128)(4,1)S(1)} %get-tuple-element.255), kind=kLoop, calls=%fused_computation.4.clone.1 | loop fusion | flops 10484736 | bytes 10496512 | tf_op jit(solution)/shard_map/while/body/eval_jaxpr/reduce_sum | solution.py:41
  120.4 2.7 %fusion.45 = bf16[512,2,128]{0,2,1:T(8,128)(2,1)S(1)} fusion(f32[2,512,2560]{2,1,0:T(8,128)S(1)} %get-tuple-element.257, f32[2,512]{1,0:T(2,128)S(1)} %get-tuple-element.258, pred[2560]{0:T(1024)(128)(4,1)S(1)} %get-tuple-element.255, bf16[2560,2,128]{0,2,1:T(8,128)(2,1)S(1)} %bitcast.79, bf16[2560,2,128]{0,2,1:T(8,128)(2,1)S(1)} %bitcast.78, ...), kind=kOutput, calls=%fused_computation.15.clone.1 | convolution fusion | flops 682491904 | bytes 13382656 | tf_op jit(solution)/shard_map/while/body/eval_jaxpr/hqk,khd->qhd/dot_general | solution.py:42
  127.8 1.3 iota_compare_fusion.3
  130.8 1.7 fusion.43
  132.5 2.2 %fusion.44 = f32[2,512]{1,0:T(2,128)S(1)} fusion(f32[2,512,2560]{2,1,0:T(8,128)S(1)} %get-tuple-element.257, f32[2,512]{1,0:T(2,128)S(1)} %get-tuple-element.258, pred[2560]{0:T(1024)(128)(4,1)S(1)} %get-tuple-element.255), kind=kLoop, calls=%fused_computation.4.clone.1 | loop fusion | flops 10484736 | bytes 10496512 | tf_op jit(solution)/shard_map/while/body/eval_jaxpr/reduce_sum | solution.py:41
  134.8 2.7 %fusion.45 = bf16[512,2,128]{0,2,1:T(8,128)(2,1)S(1)} fusion(f32[2,512,2560]{2,1,0:T(8,128)S(1)} %get-tuple-element.257, f32[2,512]{1,0:T(2,128)S(1)} %get-tuple-element.258, pred[2560]{0:T(1024)(128)(4,1)S(1)} %get-tuple-element.255, bf16[2560,2,128]{0,2,1:T(8,128)(2,1)S(1)} %bitcast.79, bf16[2560,2,128]{0,2,1:T(8,128)(2,1)S(1)} %bitcast.78, ...), kind=kOutput, calls=%fused_computation.15.clone.1 | convolution fusion | flops 682491904 | bytes 13382656 | tf_op jit(solution)/shard_map/while/body/eval_jaxpr/hqk,khd->qhd/dot_general | solution.py:42
  142.1 1.3 iota_compare_fusion.3
  145.2 1.7 fusion.43
  146.9 2.2 %fusion.44 = f32[2,512]{1,0:T(2,128)S(1)} fusion(f32[2,512,2560]{2,1,0:T(8,128)S(1)} %get-tuple-element.257, f32[2,512]{1,0:T(2,128)S(1)} %get-tuple-element.258, pred[2560]{0:T(1024)(128)(4,1)S(1)} %get-tuple-element.255), kind=kLoop, calls=%fused_computation.4.clone.1 | loop fusion | flops 10484736 | bytes 10496512 | tf_op jit(solution)/shard_map/while/body/eval_jaxpr/reduce_sum | solution.py:41
  149.2 2.7 %fusion.45 = bf16[512,2,128]{0,2,1:T(8,128)(2,1)S(1)} fusion(f32[2,512,2560]{2,1,0:T(8,128)S(1)} %get-tuple-element.257, f32[2,512]{1,0:T(2,128)S(1)} %get-tuple-element.258, pred[2560]{0:T(1024)(128)(4,1)S(1)} %get-tuple-element.255, bf16[2560,2,128]{0,2,1:T(8,128)(2,1)S(1)} %bitcast.79, bf16[2560,2,128]{0,2,1:T(8,128)(2,1)S(1)} %bitcast.78, ...), kind=kOutput, calls=%fused_computation.15.clone.1 | convolution fusion | flops 682491904 | bytes 13382656 | tf_op jit(solution)/shard_map/while/body/eval_jaxpr/hqk,khd->qhd/dot_general | solution.py:42
  159.5 1.7 fusion.43
  161.3 2.2 %fusion.44 = f32[2,512]{1,0:T(2,128)S(1)} fusion(f32[2,512,2560]{2,1,0:T(8,128)S(1)} %get-tuple-element.257, f32[2,512]{1,0:T(2,128)S(1)} %get-tuple-element.258, pred[2560]{0:T(1024)(128)(4,1)S(1)} %get-tuple-element.255), kind=kLoop, calls=%fused_computation.4.clone.1 | loop fusion | flops 10484736 | bytes 10496512 | tf_op jit(solution)/shard_map/while/body/eval_jaxpr/reduce_sum | solution.py:41
  163.5 2.7 %fusion.45 = bf16[512,2,128]{0,2,1:T(8,128)(2,1)S(1)} fusion(f32[2,512,2560]{2,1,0:T(8,128)S(1)} %get-tuple-element.257, f32[2,512]{1,0:T(2,128)S(1)} %get-tuple-element.258, pred[2560]{0:T(1024)(128)(4,1)S(1)} %get-tuple-element.255, bf16[2560,2,128]{0,2,1:T(8,128)(2,1)S(1)} %bitcast.79, bf16[2560,2,128]{0,2,1:T(8,128)(2,1)S(1)} %bitcast.78, ...), kind=kOutput, calls=%fused_computation.15.clone.1 | convolution fusion | flops 682491904 | bytes 13382656 | tf_op jit(solution)/shard_map/while/body/eval_jaxpr/hqk,khd->qhd/dot_general | solution.py:42
  173.9 1.7 fusion.43
  175.6 2.2 %fusion.44 = f32[2,512]{1,0:T(2,128)S(1)} fusion(f32[2,512,2560]{2,1,0:T(8,128)S(1)} %get-tuple-element.257, f32[2,512]{1,0:T(2,128)S(1)} %get-tuple-element.258, pred[2560]{0:T(1024)(128)(4,1)S(1)} %get-tuple-element.255), kind=kLoop, calls=%fused_computation.4.clone.1 | loop fusion | flops 10484736 | bytes 10496512 | tf_op jit(solution)/shard_map/while/body/eval_jaxpr/reduce_sum | solution.py:41
  177.9 2.7 %fusion.45 = bf16[512,2,128]{0,2,1:T(8,128)(2,1)S(1)} fusion(f32[2,512,2560]{2,1,0:T(8,128)S(1)} %get-tuple-element.257, f32[2,512]{1,0:T(2,128)S(1)} %get-tuple-element.258, pred[2560]{0:T(1024)(128)(4,1)S(1)} %get-tuple-element.255, bf16[2560,2,128]{0,2,1:T(8,128)(2,1)S(1)} %bitcast.79, bf16[2560,2,128]{0,2,1:T(8,128)(2,1)S(1)} %bitcast.78, ...), kind=kOutput, calls=%fused_computation.15.clone.1 | convolution fusion | flops 682491904 | bytes 13382656 | tf_op jit(solution)/shard_map/while/body/eval_jaxpr/hqk,khd->qhd/dot_general | solution.py:42
  181.5 39.3 %all_to_all.76 = bf16[16,160,256]{2,1,0:T(8,128)(2,1)S(1)} all-to-all(bf16[16,160,256]{2,1,0:T(8,128)(2,1)} %bitcast.80), channel_id=1, replica_groups=mesh['groups'=2,'seq'=16] {'seq'}, dimensions={0} | all-to-all | bytes 2621440 | tf_op jit(solution)/shard_map/all_to_all | solution.py:50
  (71 shorter events, 25.6 us)
Async XLA Ops:
  2.5 7.5 %copy-start.1 = (bf16[160,4096]{1,0:T(8,128)(2,1)S(1)}, bf16[160,4096]{1,0:T(8,128)(2,1)}, u32[]{:S(2)}) copy-start(bf16[160,4096]{1,0:T(8,128)(2,1)} %param.10) | copy-start | bytes 3932164
  2.5 35.3 %all-to-all-start = ((bf16[160,16,256]{2,0,1:T(8,128)(2,1)}), bf16[160,16,256]{2,0,1:T(8,128)(2,1)S(1)}, u32[]{:S(2)}, u32[]{:S(2)}) async-start(bf16[160,16,256]{2,0,1:T(8,128)(2,1)} %bitcast.41), calls=%async_computation | async-start | bytes 2621440 | tf_op jit(solution)/shard_map/all_to_all | solution.py:15
  37.8 35.3 %all-to-all-start.2 = ((bf16[160,16,256]{2,0,1:T(8,128)(2,1)}), bf16[160,16,256]{2,0,1:T(8,128)(2,1)S(1)}, u32[]{:S(2)}, u32[]{:S(2)}) async-start(bf16[160,16,256]{2,0,1:T(8,128)(2,1)} %bitcast.73), calls=%async_computation.2 | async-start | bytes 2621440 | tf_op jit(solution)/shard_map/all_to_all | solution.py:14
  73.1 1.1 copy-start
  74.2 35.4 %all-to-all-start.1 = ((bf16[160,16,256]{2,0,1:T(8,128)(2,1)}), bf16[160,16,256]{2,0,1:T(8,128)(2,1)}, u32[]{:S(2)}, u32[]{:S(2)}) async-start(bf16[160,16,256]{2,0,1:T(8,128)(2,1)} %bitcast.72), calls=%async_computation.1 | async-start | bytes 2621440 | tf_op jit(solution)/shard_map/all_to_all | solution.py:13
  84.1 1.6 copy-start.4
  87.5 22.2 %copy-start.5 = (s32[5]{0:T(128)S(1)}, s32[5]{0:T(128)}, u32[]{:S(2)}) copy-start(s32[5]{0:T(128)} %param.15) | copy-start | bytes 64
  118.1 2.3 %copy-start.2 = (bf16[2560,256]{0,1:T(8,128)(2,1)S(1)}, bf16[2560,256]{0,1:T(8,128)(2,1)}, u32[]{:S(2)}) copy-start(bf16[2560,256]{0,1:T(8,128)(2,1)} %get-tuple-element.297) | copy-start | bytes 3932164 | tf_op jit(solution)/shard_map/while
  118.2 2.3 %copy-start.3 = (bf16[2560,256]{0,1:T(8,128)(2,1)S(1)}, bf16[2560,256]{0,1:T(8,128)(2,1)}, u32[]{:S(2)}) copy-start(bf16[2560,256]{0,1:T(8,128)(2,1)} %get-tuple-element.296) | copy-start | bytes 3932164 | tf_op jit(solution)/shard_map/while
  132.5 2.3 %copy-start.2 = (bf16[2560,256]{0,1:T(8,128)(2,1)S(1)}, bf16[2560,256]{0,1:T(8,128)(2,1)}, u32[]{:S(2)}) copy-start(bf16[2560,256]{0,1:T(8,128)(2,1)} %get-tuple-element.297) | copy-start | bytes 3932164 | tf_op jit(solution)/shard_map/while
  132.5 2.3 %copy-start.3 = (bf16[2560,256]{0,1:T(8,128)(2,1)S(1)}, bf16[2560,256]{0,1:T(8,128)(2,1)}, u32[]{:S(2)}) copy-start(bf16[2560,256]{0,1:T(8,128)(2,1)} %get-tuple-element.296) | copy-start | bytes 3932164 | tf_op jit(solution)/shard_map/while
  146.9 2.3 %copy-start.2 = (bf16[2560,256]{0,1:T(8,128)(2,1)S(1)}, bf16[2560,256]{0,1:T(8,128)(2,1)}, u32[]{:S(2)}) copy-start(bf16[2560,256]{0,1:T(8,128)(2,1)} %get-tuple-element.297) | copy-start | bytes 3932164 | tf_op jit(solution)/shard_map/while
  146.9 2.3 %copy-start.3 = (bf16[2560,256]{0,1:T(8,128)(2,1)S(1)}, bf16[2560,256]{0,1:T(8,128)(2,1)}, u32[]{:S(2)}) copy-start(bf16[2560,256]{0,1:T(8,128)(2,1)} %get-tuple-element.296) | copy-start | bytes 3932164 | tf_op jit(solution)/shard_map/while
  161.3 2.3 %copy-start.2 = (bf16[2560,256]{0,1:T(8,128)(2,1)S(1)}, bf16[2560,256]{0,1:T(8,128)(2,1)}, u32[]{:S(2)}) copy-start(bf16[2560,256]{0,1:T(8,128)(2,1)} %get-tuple-element.297) | copy-start | bytes 3932164 | tf_op jit(solution)/shard_map/while
  161.3 2.3 %copy-start.3 = (bf16[2560,256]{0,1:T(8,128)(2,1)S(1)}, bf16[2560,256]{0,1:T(8,128)(2,1)}, u32[]{:S(2)}) copy-start(bf16[2560,256]{0,1:T(8,128)(2,1)} %get-tuple-element.296) | copy-start | bytes 3932164 | tf_op jit(solution)/shard_map/while
  175.6 2.3 %copy-start.2 = (bf16[2560,256]{0,1:T(8,128)(2,1)S(1)}, bf16[2560,256]{0,1:T(8,128)(2,1)}, u32[]{:S(2)}) copy-start(bf16[2560,256]{0,1:T(8,128)(2,1)} %get-tuple-element.297) | copy-start | bytes 3932164 | tf_op jit(solution)/shard_map/while
  175.6 2.3 %copy-start.3 = (bf16[2560,256]{0,1:T(8,128)(2,1)S(1)}, bf16[2560,256]{0,1:T(8,128)(2,1)}, u32[]{:S(2)}) copy-start(bf16[2560,256]{0,1:T(8,128)(2,1)} %get-tuple-element.296) | copy-start | bytes 3932164 | tf_op jit(solution)/shard_map/while
where the time goes:
time: 223 us; the launch traced here: 222 us
  waiting for transfers between devices  72.5 us (33%)
  blocking collectives  39.3 us (18%)
  local copies, waits for them, and re-layouts  35.2 us (16%)
  starting transfers between devices  22.4 us (10%)
  matrix products  22.2 us (10%)
  other arithmetic  17.6 us (8%)
  loops' own time  12.7 us (6%)
    all_to_all x1, blocking collectives, shards(): lax.all_to_all(gathered, 'seq', split_axis=0, concat_axis=1, tiled=True)  39.3 us
    all_to_all x1, waiting for transfers between devices, shards(): lax.all_to_all(v_fresh, 'seq', split_axis=1, concat_axis=0, tiled=True)  26.6 us
    all_to_all x1, waiting for transfers between devices, shards(): lax.all_to_all(k_fresh, 'seq', split_axis=1, concat_axis=0, tiled=True)  25.3 us
    all_to_all x1, waiting for transfers between devices, shards(): lax.all_to_all(q_fresh, 'seq', split_axis=1, concat_axis=0, tiled=True)  20.6 us
    dot_general x5, matrix products, one_patch(): jnp.einsum('hqk,khd->qhd', weight.astype(jnp.bfloat16), values, preferred...  13.6 us
    another operation x1, loops' own time, shards(): pieces = lax.map(one_patch, jnp.arange(patch_count, dtype=jnp.int32))  12.7 us
    reduce_sum x5, other arithmetic, one_patch(): denominator = jnp.sum(weight, axis=2)  11.2 us
    dot_general x5, matrix products, one_patch(): jnp.einsum('qhd,khd->hqk', block, keys, preferred_element_type=jnp.float32)  8.59 us
  transfers between devices with their start and end apart: 3, of which 3 were waited for; matrix products, arithmetic and copies ran while one was open for 5% of the time, Pallas kernels for 0%

commit v1 on v0

--- a/solution.py
+++ b/solution.py
@@ -12,7 +12,12 @@
     queries, keys_new, values_new = (
         lax.all_to_all(q_fresh, "seq", split_axis=1, concat_axis=0, tiled=True),
         lax.all_to_all(k_fresh, "seq", split_axis=1, concat_axis=0, tiled=True),
-        lax.all_to_all(v_fresh, "seq", split_axis=1, concat_axis=0, tiled=True),
+        jnp.concatenate(
+            lax.all_to_all(
+                jnp.stack(jnp.split(v_fresh, lax.axis_size("seq"), axis=1)), "seq", 0, 0
+            ),
+            axis=0,
+        ),
     )
     total_rows = queries.shape[0]
     width = queries.shape[1]

time: 223 us -> 245 us (1.099)
  local copies, waits for them, and re-layouts: 35.2 us -> 57.1 us
    unnamed x12 -> x27, local copies, waits for them, and re-layouts: 8.36 us -> 31.3 us
    all_to_all x1 -> x0, local copies, waits for them, and re-layouts: 2.51 us -> none  [shards(): lax.all_to_all(v_fresh, 'seq', split_axis=1, concat_axis=0, tiled=True)]
where the time goes in v1:
time: 245 us; the launch traced here: 244 us
  waiting for transfers between devices  72.5 us (30%)
  local copies, waits for them, and re-layouts  57.1 us (23%)
  blocking collectives  39.3 us (16%)
  starting transfers between devices  22.4 us (9%)
  matrix products  22.2 us (9%)
  other arithmetic  17.6 us (7%)
  loops' own time  12.8 us (5%)
    all_to_all x1, blocking collectives, shards(): lax.all_to_all(gathered, 'seq', split_axis=0, concat_axis=1, tiled=True)  39.3 us
    unnamed x27, local copies, waits for them, and re-layouts  31.3 us
    all_to_all x1, waiting for transfers between devices, shards(): lax.all_to_all(jnp.stack(jnp.split(v_fresh, lax.axis_size('seq'), axis=1)...  26.6 us
    all_to_all x1, waiting for transfers between devices, shards(): lax.all_to_all(k_fresh, 'seq', split_axis=1, concat_axis=0, tiled=True)  25.3 us
    all_to_all x1, waiting for transfers between devices, shards(): lax.all_to_all(q_fresh, 'seq', split_axis=1, concat_axis=0, tiled=True)  20.6 us
    dot_general x5, matrix products, one_patch(): jnp.einsum('hqk,khd->qhd', weight.astype(jnp.bfloat16), values, preferred...  13.6 us
    another operation x1, loops' own time, shards(): pieces = lax.map(one_patch, jnp.arange(patch_count, dtype=jnp.int32))  12.8 us
    reduce_sum x5, other arithmetic, one_patch(): denominator = jnp.sum(weight, axis=2)  11.2 us
  transfers between devices with their start and end apart: 3, of which 3 were waited for; matrix products, arithmetic and copies ran while one was open for 5% of the time, Pallas kernels for 0%

profile of v1, /device:TPU:1, one launch (start us, length us, event | category | flops | bytes accessed | tf_op | source)
XLA Modules:
  0.0 243.9 jit_solution(10480382787907858958)
XLA Ops:
  0.0 1.5 bitcast_dynamic-update-slice_fusion.15
  1.5 1.5 bitcast_dynamic-update-slice_fusion.14
  3.1 1.5 bitcast_dynamic-update-slice_fusion.13
  4.6 1.5 bitcast_dynamic-update-slice_fusion.12
  24.4 7.5 %all-to-all-start = ((bf16[16,160,256]{2,1,0:T(8,128)(2,1)}), bf16[16,160,256]{2,1,0:T(8,128)(2,1)S(1)}, u32[]{:S(2)}, u32[]{:S(2)}) async-start(bf16[16,160,256]{2,1,0:T(8,128)(2,1)} %bitcast_dynamic-update-slice_fusion), calls=%async_computation | async-start | bytes 2621440 | tf_op jit(solution)/shard_map/all_to_all | solution.py:16
  33.1 26.6 %all-to-all-done = bf16[16,160,256]{2,1,0:T(8,128)(2,1)S(1)} async-done(((bf16[16,160,256]{2,1,0:T(8,128)(2,1)}), bf16[16,160,256]{2,1,0:T(8,128)(2,1)S(1)}, u32[]{:S(2)}, u32[]{:S(2)}) %all-to-all-start) | async-done | bytes 1310752 | tf_op jit(solution)/shard_map/all_to_all | solution.py:16
  59.7 7.5 %all-to-all-start.2 = ((bf16[160,16,256]{2,0,1:T(8,128)(2,1)}), bf16[160,16,256]{2,0,1:T(8,128)(2,1)S(1)}, u32[]{:S(2)}, u32[]{:S(2)}) async-start(bf16[160,16,256]{2,0,1:T(8,128)(2,1)} %bitcast.99), calls=%async_computation.2 | async-start | bytes 2621440 | tf_op jit(solution)/shard_map/all_to_all | solution.py:14
  67.2 2.5 %copy.76 = bf16[20,16,8,256]{3,2,0,1:T(8,128)(2,1)} copy(bf16[20,16,8,256]{3,2,1,0:T(8,128)(2,1)} %bitcast.102) | data formatting | bytes 2621440 | tf_op jit(solution)/shard_map/all_to_all | solution.py:13
  69.7 25.3 %all-to-all-done.2 = bf16[160,16,256]{2,0,1:T(8,128)(2,1)S(1)} async-done(((bf16[160,16,256]{2,0,1:T(8,128)(2,1)}), bf16[160,16,256]{2,0,1:T(8,128)(2,1)S(1)}, u32[]{:S(2)}, u32[]{:S(2)}) %all-to-all-start.2) | async-done | bytes 1310752 | tf_op jit(solution)/shard_map/all_to_all | solution.py:14
  96.2 7.5 %all-to-all-start.1 = ((bf16[160,16,256]{2,0,1:T(8,128)(2,1)}), bf16[160,16,256]{2,0,1:T(8,128)(2,1)}, u32[]{:S(2)}, u32[]{:S(2)}) async-start(bf16[160,16,256]{2,0,1:T(8,128)(2,1)} %bitcast.98), calls=%async_computation.1 | async-start | bytes 2621440 | tf_op jit(solution)/shard_map/all_to_all | solution.py:13
  103.6 2.4 copy.59
  106.1 1.6 copy.62
  107.8 1.6 copy.58
  109.4 1.6 copy.61
  111.0 20.6 %all-to-all-done.1 = bf16[160,16,256]{2,0,1:T(8,128)(2,1)} async-done(((bf16[160,16,256]{2,0,1:T(8,128)(2,1)}), bf16[160,16,256]{2,0,1:T(8,128)(2,1)}, u32[]{:S(2)}, u32[]{:S(2)}) %all-to-all-start.1) | async-done | bytes 1310752 | tf_op jit(solution)/shard_map/all_to_all | solution.py:13
  131.6 71.8 %while.11 = (s32[]{:T(128)}, bf16[5,512,256]{2,1,0:T(8,128)(2,1)}, s32[5]{0:T(128)S(1)}, s32[5]{0:T(128)S(1)}, s32[2560]{0:T(1024)S(1)}, /*index=5*/bf16[2560,25...) while((s32[]{:T(128)}, bf16[5,512,256]{2,1,0:T(8,128)(2,1)}, ...), condition=%wide.region_4.5_spmd.clone, body=%wide.region_1.4_spmd.clone.sunk | while | flops 1372589056 | bytes 49856844 | solution.py:53
  138.4 1.7 fusion.43
  140.1 2.2 fusion.44
  142.3 2.7 %fusion.45 = bf16[512,2,128]{0,2,1:T(8,128)(2,1)S(1)} fusion(f32[2,512,2560]{2,1,0:T(8,128)S(1)} %get-tuple-element.257, f32[2,512]{1,0:T(2,128)S(1)} %get-tuple-element.258, pred[2560]{0:T(1024)(128)(4,1)S(1)} %get-tuple-element.255, bf16[2560,2,128]{0,2,1:T(8,128)(2,1)S(1)} %bitcast.104, bf16[2560,2,128]{0,2,1:T(8,128)(2,1)S(1)} %bitcast.103, ...), kind=kOutput, calls=%fused_computation.15.clone.1 | convolution fusion | flops 682491904 | bytes 13382656 | tf_op jit(solution)/shard_map/while/body/eval_jaxpr/hqk,khd->qhd/dot_general | solution.py:47
  152.7 1.7 fusion.43
  154.5 2.2 fusion.44
  156.7 2.7 %fusion.45 = bf16[512,2,128]{0,2,1:T(8,128)(2,1)S(1)} fusion(f32[2,512,2560]{2,1,0:T(8,128)S(1)} %get-tuple-element.257, f32[2,512]{1,0:T(2,128)S(1)} %get-tuple-element.258, pred[2560]{0:T(1024)(128)(4,1)S(1)} %get-tuple-element.255, bf16[2560,2,128]{0,2,1:T(8,128)(2,1)S(1)} %bitcast.104, bf16[2560,2,128]{0,2,1:T(8,128)(2,1)S(1)} %bitcast.103, ...), kind=kOutput, calls=%fused_computation.15.clone.1 | convolution fusion | flops 682491904 | bytes 13382656 | tf_op jit(solution)/shard_map/while/body/eval_jaxpr/hqk,khd->qhd/dot_general | solution.py:47
  167.1 1.7 fusion.43
  168.8 2.2 fusion.44
  171.1 2.7 %fusion.45 = bf16[512,2,128]{0,2,1:T(8,128)(2,1)S(1)} fusion(f32[2,512,2560]{2,1,0:T(8,128)S(1)} %get-tuple-element.257, f32[2,512]{1,0:T(2,128)S(1)} %get-tuple-element.258, pred[2560]{0:T(1024)(128)(4,1)S(1)} %get-tuple-element.255, bf16[2560,2,128]{0,2,1:T(8,128)(2,1)S(1)} %bitcast.104, bf16[2560,2,128]{0,2,1:T(8,128)(2,1)S(1)} %bitcast.103, ...), kind=kOutput, calls=%fused_computation.15.clone.1 | convolution fusion | flops 682491904 | bytes 13382656 | tf_op jit(solution)/shard_map/while/body/eval_jaxpr/hqk,khd->qhd/dot_general | solution.py:47
  181.5 1.7 fusion.43
  183.2 2.2 fusion.44
  185.4 2.7 %fusion.45 = bf16[512,2,128]{0,2,1:T(8,128)(2,1)S(1)} fusion(f32[2,512,2560]{2,1,0:T(8,128)S(1)} %get-tuple-element.257, f32[2,512]{1,0:T(2,128)S(1)} %get-tuple-element.258, pred[2560]{0:T(1024)(128)(4,1)S(1)} %get-tuple-element.255, bf16[2560,2,128]{0,2,1:T(8,128)(2,1)S(1)} %bitcast.104, bf16[2560,2,128]{0,2,1:T(8,128)(2,1)S(1)} %bitcast.103, ...), kind=kOutput, calls=%fused_computation.15.clone.1 | convolution fusion | flops 682491904 | bytes 13382656 | tf_op jit(solution)/shard_map/while/body/eval_jaxpr/hqk,khd->qhd/dot_general | solution.py:47
  195.8 1.7 fusion.43
  197.6 2.2 fusion.44
  199.8 2.7 %fusion.45 = bf16[512,2,128]{0,2,1:T(8,128)(2,1)S(1)} fusion(f32[2,512,2560]{2,1,0:T(8,128)S(1)} %get-tuple-element.257, f32[2,512]{1,0:T(2,128)S(1)} %get-tuple-element.258, pred[2560]{0:T(1024)(128)(4,1)S(1)} %get-tuple-element.255, bf16[2560,2,128]{0,2,1:T(8,128)(2,1)S(1)} %bitcast.104, bf16[2560,2,128]{0,2,1:T(8,128)(2,1)S(1)} %bitcast.103, ...), kind=kOutput, calls=%fused_computation.15.clone.1 | convolution fusion | flops 682491904 | bytes 13382656 | tf_op jit(solution)/shard_map/while/body/eval_jaxpr/hqk,khd->qhd/dot_general | solution.py:47
  203.4 39.3 %all_to_all.62 = bf16[16,160,256]{2,1,0:T(8,128)(2,1)S(1)} all-to-all(bf16[16,160,256]{2,1,0:T(8,128)(2,1)} %bitcast.105), channel_id=1, replica_groups=mesh['groups'=2,'seq'=16] {'seq'}, dimensions={0} | all-to-all | bytes 2621440 | tf_op jit(solution)/shard_map/all_to_all | solution.py:55
  (86 shorter events, 47.7 us)
Async XLA Ops:
  24.4 7.5 %copy-start.1 = (bf16[160,4096]{1,0:T(8,128)(2,1)S(1)}, bf16[160,4096]{1,0:T(8,128)(2,1)}, u32[]{:S(2)}) copy-start(bf16[160,4096]{1,0:T(8,128)(2,1)} %param.10) | copy-start | bytes 3932164
  24.4 35.3 %all-to-all-start = ((bf16[16,160,256]{2,1,0:T(8,128)(2,1)}), bf16[16,160,256]{2,1,0:T(8,128)(2,1)S(1)}, u32[]{:S(2)}, u32[]{:S(2)}) async-start(bf16[16,160,256]{2,1,0:T(8,128)(2,1)} %bitcast_dynamic-update-slice_fusion), calls=%async_computation | async-start | bytes 2621440 | tf_op jit(solution)/shard_map/all_to_all | solution.py:16
  59.7 35.3 %all-to-all-start.2 = ((bf16[160,16,256]{2,0,1:T(8,128)(2,1)}), bf16[160,16,256]{2,0,1:T(8,128)(2,1)S(1)}, u32[]{:S(2)}, u32[]{:S(2)}) async-start(bf16[160,16,256]{2,0,1:T(8,128)(2,1)} %bitcast.99), calls=%async_computation.2 | async-start | bytes 2621440 | tf_op jit(solution)/shard_map/all_to_all | solution.py:14
  95.0 1.1 copy-start
  96.2 35.4 %all-to-all-start.1 = ((bf16[160,16,256]{2,0,1:T(8,128)(2,1)}), bf16[160,16,256]{2,0,1:T(8,128)(2,1)}, u32[]{:S(2)}, u32[]{:S(2)}) async-start(bf16[160,16,256]{2,0,1:T(8,128)(2,1)} %bitcast.98), calls=%async_computation.1 | async-start | bytes 2621440 | tf_op jit(solution)/shard_map/all_to_all | solution.py:13
  106.1 1.6 copy-start.4
  109.4 22.2 %copy-start.5 = (s32[5]{0:T(128)S(1)}, s32[5]{0:T(128)}, u32[]{:S(2)}) copy-start(s32[5]{0:T(128)} %param.15) | copy-start | bytes 64
  140.1 2.3 copy-start.2
  140.1 2.3 copy-start.3
  154.4 2.3 copy-start.2
  154.4 2.3 copy-start.3
  168.8 2.3 copy-start.2
  168.8 2.3 copy-start.3
  183.2 2.3 copy-start.2
  183.2 2.3 copy-start.3
  197.5 2.3 copy-start.2
  197.5 2.3 copy-start.3
